TPU v7x, 32 devices: a whole 2x2x4 slice. The times are simulated.
32 devices in a mesh: grp: 2 (over x), seq: 4 (over y, core), head: 4 (over z).
Axes of the slice: x: 2, y: 2, z: 4, core: 2. Of those that a mesh axis runs over, the one named last changes fastest.
Arguments:
- queries: bfloat16 [256, 4096], P(('grp', 'seq'), 'head'), parts along dimension 0, may hold values from -6 to 6
- root_keys: bfloat16 [8192, 4096], P(('grp', 'seq'), 'head'), parts along dimension 0, may hold values from -6 to 6
- root_values: bfloat16 [8192, 4096], P(('grp', 'seq'), 'head'), parts along dimension 0, may hold values from -6 to 6
- branch_keys: bfloat16 [8192, 4096], P(('grp', 'seq'), 'head'), parts along dimension 0, may hold values from -6 to 6
- branch_values: bfloat16 [8192, 4096], P(('grp', 'seq'), 'head'), parts along dimension 0, may hold values from -6 to 6
- branch_lengths: int32 [8], P(('grp', 'seq')), parts along dimension 0, may hold values from 1 to 1024, 2560 in all
- branch_ids: int32 [256], P('grp'), parts along dimension 0, may hold values from 0 to 3
- slopes: float32 [32], P('head'), may hold values from 0.0001953125 to 0.08
Outputs:
- attended: bfloat16 [256, 4096], P(('grp', 'seq'), 'head'), parts along dimension 0
There are 2 independent parts, one for each index of `grp`. A program takes and returns all parts, laid end to end along the dimension named above; an argument that names none is the same for every part. Nothing has to cross between parts.
Inputs may be any that keep to these rules, and one draw needn't show every extreme that they name: `branch_lengths`: the longest branch holds exactly 1024 live positions; each holds at least one.
All inputs are finite; a program needn't handle non-finite values. No bound on the sum of `branch_lengths` on one device may be relied on, other than what follows from the above.
Results may differ from a plain program's by a relative error of at most 0.0041.
Values may be sent and summed in bfloat16 or wider, within the bound.
A program may use at most 128 MiB of HBM per device.

v0:
```python
import functools

import jax
import jax.numpy as jnp
from jax import lax
from jax.experimental import pallas as pl
from jax.experimental.pallas import tpu as pltpu
from jax.sharding import PartitionSpec as P

MESH = pl.DeviceIdType.MESH
LOG2E = 1.4426950408889634
MASKED = -1e30
LANES = 128
BLOCK = 2048


def kernel(
    n,
    q_hbm,
    rk_hbm,
    rv_hbm,
    bk_hbm,
    bv_hbm,
    len_hbm,
    ids_hbm,
    slope_hbm,
    out_ref,
    len_ref,
    ids_ref,
    slope_ref,
    small_sem,
    kbuf,
    vbuf,
    kaug,
    qaug,
    q_all,
    s_buf,
    o_send,
    o_recv,
    st_cols,
    st_send,
    st_recv,
    share_buf,
    kv_sem,
    own_sem,
    q_ssem,
    q_rsem,
    o_ssem,
    o_rsem,
    st_ssem,
    st_rsem,
):
    heads = slope_hbm.shape[0]
    query_dev = q_hbm.shape[0]
    rows = q_all.shape[1]
    root_dev = rk_hbm.shape[0]
    branch_len = bk_hbm.shape[0]
    keys = root_dev + branch_len
    size = q_hbm.shape[1] // heads
    scale = 1.0 / size**0.5
    rate = scale * LOG2E
    me = lax.axis_index("seq")
    peers = [(d, lax.rem(me + d, n)) for d in range(1, n)]
    mine = pl.ds(pl.multiple_of(me * query_dev, query_dev), query_dev)

    def cols(h):
        return pl.ds(h * size, size)

    def fetch(which, h):
        source = (rk_hbm, bk_hbm, rv_hbm, bv_hbm)[which]
        landing = (kbuf, vbuf)[which // 2]
        span = (pl.ds(0, root_dev), pl.ds(root_dev, branch_len))[which % 2]
        return pltpu.make_async_copy(
            source.at[:, cols(h)], landing.at[h, span], kv_sem.at[which, h]
        )

    def own_copy(h):
        return pltpu.make_async_copy(q_hbm.at[:, cols(h)], q_all.at[h, mine], own_sem.at[h])

    def q_copy(h, d, peer):
        return pltpu.make_async_remote_copy(
            src_ref=q_hbm.at[:, cols(h)],
            dst_ref=q_all.at[h, mine],
            send_sem=q_ssem.at[d - 1],
            recv_sem=q_rsem.at[h, d - 1],
            device_id={"seq": peer},
            device_id_type=MESH,
        )

    def o_copy(h, d, peer):
        theirs = pl.ds(pl.multiple_of(peer * query_dev, query_dev), query_dev)
        return pltpu.make_async_remote_copy(
            src_ref=o_send.at[h, theirs],
            dst_ref=o_recv.at[d - 1, h],
            send_sem=o_ssem.at[d - 1],
            recv_sem=o_rsem.at[d - 1],
            device_id={"seq": peer},
            device_id_type=MESH,
        )

    def q_whole(d, peer):
        return pltpu.make_async_remote_copy(
            src_ref=q_hbm,
            dst_ref=q_hbm,
            send_sem=q_ssem.at[d - 1],
            recv_sem=q_ssem.at[d - 1],
            device_id={"seq": peer},
            device_id_type=MESH,
        )

    def o_whole(d, peer):
        theirs = pl.ds(pl.multiple_of(peer * query_dev, query_dev), query_dev)
        return pltpu.make_async_remote_copy(
            src_ref=o_send.at[:, theirs],
            dst_ref=o_recv.at[d - 1],
            send_sem=o_ssem.at[d - 1],
            recv_sem=o_rsem.at[d - 1],
            device_id={"seq": peer},
            device_id_type=MESH,
        )

    def st_copy(d, peer):
        return pltpu.make_async_remote_copy(
            src_ref=st_send,
            dst_ref=st_recv.at[d - 1],
            send_sem=st_ssem.at[d - 1],
            recv_sem=st_rsem.at[d - 1],
            device_id={"seq": peer},
            device_id_type=MESH,
        )

    barrier = pltpu.get_barrier_semaphore()
    for _, peer in peers:
        pl.semaphore_signal(barrier, inc=1, device_id={"seq": peer}, device_id_type=MESH)
    small = (
        pltpu.make_async_copy(len_hbm, len_ref, small_sem.at[0]),
        pltpu.make_async_copy(ids_hbm, ids_ref, small_sem.at[1]),
        pltpu.make_async_copy(slope_hbm, slope_ref, small_sem.at[2]),
    )
    for copy in small:
        copy.start()
    for h in range(heads):
        own_copy(h).start()
    for h in range(heads):
        for which in range(4):
            fetch(which, h).start()
    pl.semaphore_wait(barrier, n - 1)
    for h in range(heads):
        for d, peer in peers:
            q_copy(h, d, peer).start()

    for copy in small:
        copy.wait()
    span = root_dev * n + branch_len

    @pl.loop(0, keys // LANES)
    def _(i):
        start = pl.multiple_of(i * LANES, LANES)
        spot = start + lax.broadcasted_iota(jnp.int32, (LANES, LANES), 0)
        lane = lax.broadcasted_iota(jnp.int32, (LANES, LANES), 1)
        is_branch = spot >= root_dev
        back = jnp.where(is_branch, keys - spot, span - me * root_dev - spot)
        low = back & 255
        dead = is_branch & (spot - root_dev >= len_ref[0])
        aug = jnp.where(
            lane < 6,
            jnp.where(lane < 3, low - back, -low).astype(jnp.float32),
            jnp.where(
                lane == 6,
                jnp.where(dead, MASKED, 0.0),
                jnp.where((lane == 7) & is_branch, 1.0, 0.0),
            ),
        )
        kaug[pl.ds(start, LANES), :] = aug.astype(jnp.bfloat16)

    down = lax.broadcasted_iota(jnp.int32, (rows, rows), 0)
    across = lax.broadcasted_iota(jnp.int32, (rows, rows), 1)
    other = jnp.where(ids_ref[...] == me, 0.0, MASKED)
    row_mask = jnp.sum(jnp.where(down == across, other, 0.0), axis=1, keepdims=True)
    qlane = lax.broadcasted_iota(jnp.int32, (rows, LANES), 1)
    qaug[...] = jnp.where(qlane == 6, 1.0, jnp.where(qlane == 7, row_mask, 0.0))
    st_cols[...] = jnp.zeros_like(st_cols)

    def await_key(h):
        for which in (0, 1):
            fetch(which, h).wait()
        own_copy(h).wait()
        for d, peer in peers:
            q_copy(h, d, peer).wait_recv()

    def await_value(h):
        for which in (2, 3):
            fetch(which, h).wait()

    def widened(h):
        slope = jnp.full((1, LANES), slope_ref[h] * (size**0.5), jnp.float32)
        first = slope.astype(jnp.bfloat16).astype(jnp.float32)
        second = (slope - first).astype(jnp.bfloat16).astype(jnp.float32)
        third = slope - first - second
        nth = lax.rem(lax.broadcasted_iota(jnp.int32, (1, LANES), 1), 3)
        parts = jnp.where(nth == 0, first, jnp.where(nth == 1, second, third))
        extra = jnp.where(qlane < 6, parts, qaug[...]).astype(jnp.bfloat16)
        return jnp.concatenate([q_all[h], extra], axis=1)

    def folded(combine, array):
        return functools.reduce(
            combine, [array[:, i : i + LANES] for i in range(0, array.shape[1], LANES)]
        )

    block = min(BLOCK, keys)

    def step(h_score, h_mix, top):
        query = None if h_score is None else widened(h_score)
        new_top, mixed, total = None, None, None
        for j in range(keys // block):
            at = pl.ds(j * block, block)
            if h_score is not None:
                key = jnp.concatenate([kbuf[h_score, at], kaug[at]], axis=1)
                scores = lax.dot_general(
                    query, key, (((1,), (1,)), ((), ())), preferred_element_type=jnp.float32
                )
                s_buf[h_score % 2, :, at] = scores
                high = folded(jnp.maximum, scores)
                new_top = high if new_top is None else jnp.maximum(new_top, high)
            if h_mix is not None:
                weights = jnp.exp2((s_buf[h_mix % 2, :, at] - top) * rate)
                part = folded(jnp.add, weights)
                share = jnp.dot(
                    weights.astype(jnp.bfloat16),
                    vbuf[h_mix, at],
                    preferred_element_type=jnp.float32,
                )
                mixed = share if mixed is None else mixed + share
                total = part if total is None else total + part
        if h_mix is not None:
            total = jnp.sum(total, axis=1, keepdims=True)
            level = top * rate + jnp.log(total) * LOG2E
            st_cols[...] = jnp.where(qlane == h_mix, level, st_cols[...])
            if h_mix + 1 == heads:
                st_send[...] = jnp.transpose(st_cols[...])[: st_send.shape[0]]
                for d, peer in peers:
                    st_copy(d, peer).start()
            o_send[h_mix] = (mixed / total).astype(jnp.bfloat16)
        if new_top is not None:
            return jnp.max(new_top, axis=1, keepdims=True)

    await_key(0)
    top = step(0, None, None)
    for h in range(heads):
        last = h + 1 == heads
        if not last:
            await_key(h + 1)
        await_value(h)
        top = step(None if last else h + 1, h, top)
        for d, peer in peers:
            o_copy(h, d, peer).start()
    for d, peer in peers:
        q_whole(d, peer).wait_send()
    for d, peer in peers:
        st_copy(d, peer).wait_recv()
    levels = [st_send[...]] + [st_recv[d - 1] for d, _ in peers]
    high = functools.reduce(jnp.maximum, levels)
    shares = [jnp.exp2(level - high) for level in levels]
    whole = functools.reduce(jnp.add, shares)
    deep = st_send.shape[0]
    blank = [jnp.zeros_like(whole)] * (-n % (LANES // deep))
    columns = jnp.concatenate([share / whole for share in shares] + blank, axis=0)
    share_buf[...] = jnp.transpose(columns)
    share = share_buf[mine]
    for d, peer in peers:
        o_whole(d, peer).wait_recv()
    for h in range(heads):
        total = share[:, h : h + 1] * o_send[h, mine].astype(jnp.float32)
        for d, _ in peers:
            spot = d * deep + h
            total += share[:, spot : spot + 1] * o_recv[d - 1, h].astype(jnp.float32)
        out_ref[:, cols(h)] = total.astype(out_ref.dtype)
    for d, peer in peers:
        o_whole(d, peer).wait_send()
        st_copy(d, peer).wait_send()


def shards(
    queries, root_keys, root_values, branch_keys, branch_values, branch_lengths, branch_ids, slopes
):
    n = lax.axis_size("seq")
    heads = slopes.shape[0]
    query_dev, width = queries.shape
    size = width // heads
    rows = branch_ids.shape[0]
    keys = root_keys.shape[0] + branch_keys.shape[0]
    deep = -(-heads // 8) * 8
    hbm = pl.BlockSpec(memory_space=pl.ANY)
    vmem = pl.BlockSpec(memory_space=pltpu.VMEM)
    dma = pltpu.SemaphoreType.DMA
    return pl.pallas_call(
        functools.partial(kernel, n),
        out_shape=jax.ShapeDtypeStruct((query_dev, width), jnp.bfloat16),
        in_specs=[hbm] * 8,
        out_specs=vmem,
        scratch_shapes=[
            pltpu.SMEM((1,), jnp.int32),
            pltpu.VMEM((1, rows), jnp.int32),
            pltpu.SMEM((heads,), jnp.float32),
            dma((3,)),
            pltpu.VMEM((heads, keys, size), jnp.bfloat16),
            pltpu.VMEM((heads, keys, size), jnp.bfloat16),
            pltpu.VMEM((keys, LANES), jnp.bfloat16),
            pltpu.VMEM((rows, LANES), jnp.float32),
            pltpu.VMEM((heads, rows, size), jnp.bfloat16),
            pltpu.VMEM((2, rows, keys), jnp.float32),
            pltpu.VMEM((heads, rows, size), jnp.bfloat16),
            pltpu.VMEM((n - 1, heads, query_dev, size), jnp.bfloat16),
            pltpu.VMEM((rows, LANES), jnp.float32),
            pltpu.VMEM((deep, rows), jnp.float32),
            pltpu.VMEM((n - 1, deep, rows), jnp.float32),
            pltpu.VMEM((rows, -(-n * deep // LANES) * LANES), jnp.float32),
            dma((4, heads)),
            dma((heads,)),
            dma((n - 1,)),
            dma((heads, n - 1)),
            dma((n - 1,)),
            dma((n - 1,)),
            dma((n - 1,)),
            dma((n - 1,)),
        ],
        compiler_params=pltpu.CompilerParams(
            collective_id=0, has_side_effects=True, vmem_limit_bytes=60000 * 1024
        ),
    )(
        queries,
        root_keys,
        root_values,
        branch_keys,
        branch_values,
        branch_lengths,
        branch_ids.reshape(1, rows),
        slopes,
    )


def solution(mesh):
    in_specs = (
        P(("grp", "seq"), "head"),
        P(("grp", "seq"), "head"),
        P(("grp", "seq"), "head"),
        P(("grp", "seq"), "head"),
        P(("grp", "seq"), "head"),
        P(("grp", "seq")),
        P("grp"),
        P("head"),
    )
    out_specs = P(("grp", "seq"), "head")
    return jax.shard_map(shards, mesh=mesh, in_specs=in_specs, out_specs=out_specs, check_vma=False)
```

profile of v0, /device:TPU:0, one launch (start us, length us, event | category | flops | bytes accessed | tf_op | source)
XLA Modules:
  0.0 18.3 jit_solution(5790210795780829051)
XLA Ops:
  0.7 16.1 %shard_map.82 = bf16[32,1024]{1,0:T(8,128)(2,1)} custom-call(bf16[32,1024]{1,0:T(8,128)(2,1)} %q_hbm.1, bf16[1024,1024]{1,0:T(8,128)(2,1)} %rk_hbm.1, bf16[1024,1024]{1,0:T(8,128)(2,1)} %rv_hbm.1, bf16[1024,1024]{1,0:T(8,128)(2,1)} %bk_hbm.1, bf16[1024,1024]{1,0:T(8,128)(2,1)} %bv_hbm.1, s32[1]{0:T(128)S(6)} %copy.10.len_hbm, s32[1,128]{1,0:T(1,128)} %bitcast.1, ...), custom_call_target="tpu_custom_call" | custom-call | tf_op jit(solution)/shard_map/pallas_call | solution.py:296
  16.8 1.5 %copy.11 = bf16[32,1024]{1,0:T(8,128)(2,1)} copy(bf16[32,1024]{1,0:T(8,128)(2,1)} %shard_map.82) | data formatting | bytes 131072
where the time goes:
time: 18.4 us; the launch traced here: 18.3 us
  Pallas kernels  16.1 us (88%)
  local copies, waits for them, and re-layouts  1.47 us (8%)
  between operations  0.66 us (4%)
    pallas_call x1, Pallas kernels, shards(): pl.pallas_call(functools.partial(kernel, n), out_shape=jax.ShapeDtypeStru...  16.1 us
    unnamed x1, local copies, waits for them, and re-layouts  1.47 us

commit v1 on v0

--- a/solution.py
+++ b/solution.py
@@ -12,6 +12,14 @@
 MASKED = -1e30
 LANES = 128
 BLOCK = 2048
+mark = jax.named_scope
+
+
+def group_starts(heads):
+    starts = [0, 1]
+    while starts[-1] < heads:
+        starts.append(min(2 * starts[-1], heads))
+    return starts
 
 
 def kernel(
@@ -29,8 +37,7 @@
     ids_ref,
     slope_ref,
     small_sem,
-    kbuf,
-    vbuf,
+    kv,
     kaug,
     qaug,
     q_all,
@@ -52,7 +59,7 @@
 ):
     heads = slope_hbm.shape[0]
     query_dev = q_hbm.shape[0]
-    rows = q_all.shape[1]
+    rows = q_all.shape[0]
     root_dev = rk_hbm.shape[0]
     branch_len = bk_hbm.shape[0]
     keys = root_dev + branch_len
@@ -63,58 +70,56 @@
     peers = [(d, lax.rem(me + d, n)) for d in range(1, n)]
     mine = pl.ds(pl.multiple_of(me * query_dev, query_dev), query_dev)
 
+    starts = group_starts(heads)
+
     def cols(h):
         return pl.ds(h * size, size)
 
+    def group_of(h):
+        return max(g for g in range(len(starts) - 1) if starts[g] <= h)
+
+    def span_of(g):
+        return pl.ds(starts[g] * size, (starts[g + 1] - starts[g]) * size)
+
     def fetch(which, h):
         source = (rk_hbm, bk_hbm, rv_hbm, bv_hbm)[which]
-        landing = (kbuf, vbuf)[which // 2]
         span = (pl.ds(0, root_dev), pl.ds(root_dev, branch_len))[which % 2]
         return pltpu.make_async_copy(
-            source.at[:, cols(h)], landing.at[h, span], kv_sem.at[which, h]
-        )
-
-    def own_copy(h):
-        return pltpu.make_async_copy(q_hbm.at[:, cols(h)], q_all.at[h, mine], own_sem.at[h])
-
-    def q_copy(h, d, peer):
+            source.at[:, cols(h)], kv.at[h, which // 2, span], kv_sem.at[group_of(h)]
+        )
+
+    def fetched(g):
+        some = kv.at[pl.ds(starts[g], starts[g + 1] - starts[g])]
+        return pltpu.make_async_copy(some, some, kv_sem.at[g])
+
+    own_copy = pltpu.make_async_copy(q_hbm, q_all.at[mine], own_sem.at[0])
+
+    def q_copy(g, peer):
+        part = q_all.at[mine, span_of(g)]
         return pltpu.make_async_remote_copy(
-            src_ref=q_hbm.at[:, cols(h)],
-            dst_ref=q_all.at[h, mine],
-            send_sem=q_ssem.at[d - 1],
-            recv_sem=q_rsem.at[h, d - 1],
+            src_ref=part,
+            dst_ref=part,
+            send_sem=q_ssem.at[0],
+            recv_sem=q_rsem.at[g],
             device_id={"seq": peer},
             device_id_type=MESH,
         )
+
+    def q_arrived(g):
+        part = q_all.at[pl.ds(0, rows - query_dev), span_of(g)]
+        return pltpu.make_async_copy(part, part, q_rsem.at[g])
+
+    def q_sent():
+        part = q_all.at[pl.ds(0, rows - query_dev)]
+        return pltpu.make_async_copy(part, part, q_ssem.at[0])
 
     def o_copy(h, d, peer):
         theirs = pl.ds(pl.multiple_of(peer * query_dev, query_dev), query_dev)
         return pltpu.make_async_remote_copy(
             src_ref=o_send.at[h, theirs],
             dst_ref=o_recv.at[d - 1, h],
-            send_sem=o_ssem.at[d - 1],
-            recv_sem=o_rsem.at[d - 1],
-            device_id={"seq": peer},
-            device_id_type=MESH,
-        )
-
-    def q_whole(d, peer):
-        return pltpu.make_async_remote_copy(
-            src_ref=q_hbm,
-            dst_ref=q_hbm,
-            send_sem=q_ssem.at[d - 1],
-            recv_sem=q_ssem.at[d - 1],
-            device_id={"seq": peer},
-            device_id_type=MESH,
-        )
-
-    def o_whole(d, peer):
-        theirs = pl.ds(pl.multiple_of(peer * query_dev, query_dev), query_dev)
-        return pltpu.make_async_remote_copy(
-            src_ref=o_send.at[:, theirs],
-            dst_ref=o_recv.at[d - 1],
-            send_sem=o_ssem.at[d - 1],
-            recv_sem=o_rsem.at[d - 1],
+            send_sem=o_ssem.at[0],
+            recv_sem=o_rsem.at[0],
             device_id={"seq": peer},
             device_id_type=MESH,
         )
@@ -123,11 +128,14 @@
         return pltpu.make_async_remote_copy(
             src_ref=st_send,
             dst_ref=st_recv.at[d - 1],
-            send_sem=st_ssem.at[d - 1],
-            recv_sem=st_rsem.at[d - 1],
+            send_sem=st_ssem.at[0],
+            recv_sem=st_rsem.at[0],
             device_id={"seq": peer},
             device_id_type=MESH,
         )
+
+    def drain(buffer, sem):
+        return pltpu.make_async_copy(buffer, buffer, sem.at[0])
 
     barrier = pltpu.get_barrier_semaphore()
     for _, peer in peers:
@@ -137,20 +145,22 @@
         pltpu.make_async_copy(ids_hbm, ids_ref, small_sem.at[1]),
         pltpu.make_async_copy(slope_hbm, slope_ref, small_sem.at[2]),
     )
+    own_copy.start()
     for copy in small:
         copy.start()
-    for h in range(heads):
-        own_copy(h).start()
+    own_copy.wait()
+    for copy in small:
+        copy.wait()
     for h in range(heads):
         for which in range(4):
             fetch(which, h).start()
-    pl.semaphore_wait(barrier, n - 1)
-    for h in range(heads):
-        for d, peer in peers:
-            q_copy(h, d, peer).start()
-
-    for copy in small:
-        copy.wait()
+    with mark("P_barrier"):
+        pl.semaphore_wait(barrier, n - 1)
+    with mark("P_qissue"):
+        for g in range(len(starts) - 1):
+            for _, peer in peers:
+                q_copy(g, peer).start()
+
     span = root_dev * n + branch_len
 
     @pl.loop(0, keys // LANES)
@@ -181,16 +191,10 @@
     qaug[...] = jnp.where(qlane == 6, 1.0, jnp.where(qlane == 7, row_mask, 0.0))
     st_cols[...] = jnp.zeros_like(st_cols)
 
-    def await_key(h):
-        for which in (0, 1):
-            fetch(which, h).wait()
-        own_copy(h).wait()
-        for d, peer in peers:
-            q_copy(h, d, peer).wait_recv()
-
-    def await_value(h):
-        for which in (2, 3):
-            fetch(which, h).wait()
+    def await_head(h):
+        if h in starts:
+            fetched(starts.index(h)).wait()
+            q_arrived(starts.index(h)).wait()
 
     def widened(h):
         slope = jnp.full((1, LANES), slope_ref[h] * (size**0.5), jnp.float32)
@@ -200,7 +204,7 @@
         nth = lax.rem(lax.broadcasted_iota(jnp.int32, (1, LANES), 1), 3)
         parts = jnp.where(nth == 0, first, jnp.where(nth == 1, second, third))
         extra = jnp.where(qlane < 6, parts, qaug[...]).astype(jnp.bfloat16)
-        return jnp.concatenate([q_all[h], extra], axis=1)
+        return jnp.concatenate([q_all[:, cols(h)], extra], axis=1)
 
     def folded(combine, array):
         return functools.reduce(
@@ -215,7 +219,7 @@
         for j in range(keys // block):
             at = pl.ds(j * block, block)
             if h_score is not None:
-                key = jnp.concatenate([kbuf[h_score, at], kaug[at]], axis=1)
+                key = jnp.concatenate([kv[h_score, 0, at], kaug[at]], axis=1)
                 scores = lax.dot_general(
                     query, key, (((1,), (1,)), ((), ())), preferred_element_type=jnp.float32
                 )
@@ -227,7 +231,7 @@
                 part = folded(jnp.add, weights)
                 share = jnp.dot(
                     weights.astype(jnp.bfloat16),
-                    vbuf[h_mix, at],
+                    kv[h_mix, 1, at],
                     preferred_element_type=jnp.float32,
                 )
                 mixed = share if mixed is None else mixed + share
@@ -244,20 +248,22 @@
         if new_top is not None:
             return jnp.max(new_top, axis=1, keepdims=True)
 
-    await_key(0)
-    top = step(0, None, None)
+    with mark("P_ak0"):
+        await_head(0)
+    with mark("P_s0"):
+        top = step(0, None, None)
     for h in range(heads):
         last = h + 1 == heads
         if not last:
-            await_key(h + 1)
-        await_value(h)
-        top = step(None if last else h + 1, h, top)
+            with mark("P_ak%d" % (h + 1)):
+                await_head(h + 1)
+        with mark("P_step%d" % h):
+            top = step(None if last else h + 1, h, top)
         for d, peer in peers:
             o_copy(h, d, peer).start()
-    for d, peer in peers:
-        q_whole(d, peer).wait_send()
-    for d, peer in peers:
-        st_copy(d, peer).wait_recv()
+    q_sent().wait()
+    with mark("P_st"):
+        drain(st_recv, st_rsem).wait()
     levels = [st_send[...]] + [st_recv[d - 1] for d, _ in peers]
     high = functools.reduce(jnp.maximum, levels)
     shares = [jnp.exp2(level - high) for level in levels]
@@ -267,17 +273,17 @@
     columns = jnp.concatenate([share / whole for share in shares] + blank, axis=0)
     share_buf[...] = jnp.transpose(columns)
     share = share_buf[mine]
-    for d, peer in peers:
-        o_whole(d, peer).wait_recv()
+    with mark('P_orecv'):
+        drain(o_recv, o_rsem).wait()
     for h in range(heads):
         total = share[:, h : h + 1] * o_send[h, mine].astype(jnp.float32)
         for d, _ in peers:
             spot = d * deep + h
             total += share[:, spot : spot + 1] * o_recv[d - 1, h].astype(jnp.float32)
         out_ref[:, cols(h)] = total.astype(out_ref.dtype)
-    for d, peer in peers:
-        o_whole(d, peer).wait_send()
-        st_copy(d, peer).wait_send()
+    with mark('P_osend'):
+        drain(o_recv, o_ssem).wait()
+        drain(st_recv, st_ssem).wait()
 
 
 def shards(
@@ -290,12 +296,13 @@
     rows = branch_ids.shape[0]
     keys = root_keys.shape[0] + branch_keys.shape[0]
     deep = -(-heads // 8) * 8
+    groups = len(group_starts(heads)) - 1
     hbm = pl.BlockSpec(memory_space=pl.ANY)
     vmem = pl.BlockSpec(memory_space=pltpu.VMEM)
     dma = pltpu.SemaphoreType.DMA
     return pl.pallas_call(
         functools.partial(kernel, n),
-        out_shape=jax.ShapeDtypeStruct((query_dev, width), jnp.bfloat16),
+        out_shape=pltpu.VMEM((query_dev, width), jnp.bfloat16),
         in_specs=[hbm] * 8,
         out_specs=vmem,
         scratch_shapes=[
@@ -303,11 +310,10 @@
             pltpu.VMEM((1, rows), jnp.int32),
             pltpu.SMEM((heads,), jnp.float32),
             dma((3,)),
-            pltpu.VMEM((heads, keys, size), jnp.bfloat16),
-            pltpu.VMEM((heads, keys, size), jnp.bfloat16),
+            pltpu.VMEM((heads, 2, keys, size), jnp.bfloat16),
             pltpu.VMEM((keys, LANES), jnp.bfloat16),
             pltpu.VMEM((rows, LANES), jnp.float32),
-            pltpu.VMEM((heads, rows, size), jnp.bfloat16),
+            pltpu.VMEM((rows, width), jnp.bfloat16),
             pltpu.VMEM((2, rows, keys), jnp.float32),
             pltpu.VMEM((heads, rows, size), jnp.bfloat16),
             pltpu.VMEM((n - 1, heads, query_dev, size), jnp.bfloat16),
@@ -315,14 +321,14 @@
             pltpu.VMEM((deep, rows), jnp.float32),
             pltpu.VMEM((n - 1, deep, rows), jnp.float32),
             pltpu.VMEM((rows, -(-n * deep // LANES) * LANES), jnp.float32),
-            dma((4, heads)),
-            dma((heads,)),
-            dma((n - 1,)),
-            dma((heads, n - 1)),
-            dma((n - 1,)),
-            dma((n - 1,)),
-            dma((n - 1,)),
-            dma((n - 1,)),
+            dma((groups,)),
+            dma((1,)),
+            dma((1,)),
+            dma((groups,)),
+            dma((1,)),
+            dma((1,)),
+            dma((1,)),
+            dma((1,)),
         ],
         compiler_params=pltpu.CompilerParams(
             collective_id=0, has_side_effects=True, vmem_limit_bytes=60000 * 1024

time: 18.4 us -> 16.2 us (0.88)
  Pallas kernels: 16.1 us -> 14.7 us
  local copies, waits for them, and re-layouts: 1.47 us -> 0.63 us
    pallas_call x1, Pallas kernels: 16.1 us -> 14.7 us  [shards(): pl.pallas_call(functools.partial(kernel, n), out_shape=pltpu.VMEM((query_...]
    unnamed x1, local copies, waits for them, and re-layouts: 1.47 us -> 0.63 us
where the time goes in v1:
time: 16.2 us; the launch traced here: 16 us
  Pallas kernels  14.7 us (91%)
  between operations  0.66 us (4%)
  local copies, waits for them, and re-layouts  0.63 us (4%)
    pallas_call x1, Pallas kernels, shards(): pl.pallas_call(functools.partial(kernel, n), out_shape=pltpu.VMEM((query_...  14.7 us
    unnamed x1, local copies, waits for them, and re-layouts  0.63 us

profile of v1, /device:TPU:0, one launch (start us, length us, event | category | flops | bytes accessed | tf_op | source)
XLA Modules:
  0.0 16.0 jit_solution(6503632049881983001)
XLA Ops:
  0.7 14.7 %shard_map.82 = bf16[32,1024]{1,0:T(8,128)(2,1)S(1)} custom-call(bf16[32,1024]{1,0:T(8,128)(2,1)} %q_hbm.1, bf16[1024,1024]{1,0:T(8,128)(2,1)} %rk_hbm.1, bf16[1024,1024]{1,0:T(8,128)(2,1)} %rv_hbm.1, bf16[1024,1024]{1,0:T(8,128)(2,1)} %bk_hbm.1, bf16[1024,1024]{1,0:T(8,128)(2,1)} %bv_hbm.1, s32[1]{0:T(128)S(6)} %copy.11.len_hbm, s32[1,128]{1,0:T(1,128)} %bitcast.1, ...), custom_call_target="tpu_custom_call" | custom-call | tf_op jit(solution)/shard_map/pallas_call | solution.py:303
  15.4 0.6 %copy.10 = bf16[32,1024]{1,0:T(8,128)(2,1)} copy(bf16[32,1024]{1,0:T(8,128)(2,1)S(1)} %shard_map.82) | data formatting | bytes 131072
